TPU v7x, 32 devices: a whole 2x2x4 slice. The times are simulated.
32 devices in a mesh: ctx: 16 (over z, y, x), head: 2 (over core).
Axes of the slice: x: 2, y: 2, z: 4, core: 2. Of those that a mesh axis runs over, the one named last changes fastest.
Arguments:
- queries: bfloat16 [512, 8192], P('ctx', 'head'), may hold values from -6 to 6
- cache_keys: bfloat16 [16384, 8, 128], P('ctx', 'head'), may hold values from -6 to 6
- cache_values: bfloat16 [16384, 8, 128], P('ctx', 'head'), may hold values from -6 to 6
- vertical_blocks: int32 [64, 8], P('head'), may hold values from 0 to 127, as said below
- slash_offsets: int32 [64, 48], P('head'), may hold values from 0 to 127, as said below
- out_weight: bfloat16 [8192, 8192], P('head', 'ctx'), may hold values from -0.0625 to 0.0625
Outputs:
- projected: bfloat16 [512, 8192], P('head', 'ctx')
Inputs may be any that keep to these rules, and one draw needn't show every extreme that they name: `vertical_blocks`: every head's list holds block 0; entries may repeat, and a block counts once however often it is named. `slash_offsets`: every head's list holds offset 0; entries may repeat, and a block counts once however often it is reached.
All inputs are finite; a program needn't handle non-finite values.
Results may differ from a plain program's by a relative error of at most 0.007.
Values may be sent and summed in bfloat16 or wider, within the bound.
No kernel may reach another device: no remote copies, remote signals or barrier semaphores. Data moves between devices by JAX's collectives and lax.ppermute only.
A program may use at most 128 MiB of HBM per device.

v0:
```python
from functools import partial

import jax
import jax.numpy as jnp
from jax import lax
from jax.sharding import PartitionSpec as P

BLOCK = 128


NEG_FILL = -1e30


def block_terms(q_four, key_block, value_block, allowed_mask, score_scale):
    kv_local = q_four.shape[1]
    group_size = q_four.shape[2]
    scores = (
        jnp.einsum("qgjd,kgd->qgjk", q_four, key_block, preferred_element_type=jnp.float32)
        * score_scale
    )
    scores = scores.reshape(scores.shape[0], kv_local * group_size, scores.shape[3])
    masked = jnp.where(allowed_mask, scores, NEG_FILL)
    block_peak = jnp.max(masked, axis=-1)
    safe_peak = jnp.where(block_peak > 0.5 * NEG_FILL, block_peak, 0.0)
    weights = jnp.where(allowed_mask, jnp.exp(scores - safe_peak[..., None]), 0.0).astype(
        jnp.bfloat16
    )
    block_total = jnp.sum(weights.astype(jnp.float32), axis=-1)
    weights_four = weights.reshape(weights.shape[0], kv_local, group_size, weights.shape[2])
    block_out = jnp.einsum(
        "qgjk,kgd->qgjd", weights_four, value_block, preferred_element_type=jnp.float32
    )
    return (
        block_peak,
        block_total,
        block_out.reshape(block_out.shape[0], kv_local * group_size, block_out.shape[3]),
    )


def body(queries, cache_keys, cache_values, vertical_blocks, slash_offsets, out_weight):
    ctx_count = lax.axis_size("ctx")
    ctx_place = lax.axis_index("ctx")
    q_whole = lax.all_gather(queries, "ctx", axis=0, tiled=True)
    q_total = q_whole.shape[0]
    local_len, kv_local, head_width = cache_keys.shape
    heads_local = vertical_blocks.shape[0]
    group_size = heads_local // kv_local
    local_blocks = local_len // BLOCK
    q_blocks = q_total // BLOCK
    all_blocks = local_blocks * ctx_count
    score_scale = float(head_width) ** (-0.5)
    q_four = q_whole.reshape(q_total, kv_local, group_size, head_width)
    block_ids = ctx_place * local_blocks + jnp.arange(local_blocks, dtype=jnp.int32)
    query_blocks = all_blocks - q_blocks + jnp.arange(q_blocks, dtype=jnp.int32)
    vertical_hit = jnp.any(vertical_blocks[:, :, None] == block_ids[None, None, :], axis=1)
    offsets = query_blocks[:, None] - block_ids[None, :]
    slash_hit = jnp.any(slash_offsets[:, None, None, :] == offsets[None, :, :, None], axis=3)
    chosen = jnp.transpose(vertical_hit[:, None, :] | slash_hit, (1, 0, 2))
    first_query = all_blocks * BLOCK - q_total
    query_pos = first_query + jnp.arange(q_total, dtype=jnp.int32)

    def visit_block(turn_index, state_carry, block_order):
        run_peak, run_total, run_out = state_carry
        local_block = block_order[turn_index]
        key_block = lax.dynamic_slice_in_dim(cache_keys, local_block * BLOCK, BLOCK, 0)
        value_block = lax.dynamic_slice_in_dim(cache_values, local_block * BLOCK, BLOCK, 0)
        picked = lax.dynamic_index_in_dim(chosen, local_block, 2, keepdims=False)
        picked_rows = jnp.repeat(picked, BLOCK, axis=0)
        key_pos = ctx_place * local_len + local_block * BLOCK + jnp.arange(BLOCK, dtype=jnp.int32)
        allowed_mask = picked_rows[:, :, None] & (
            key_pos[None, None, :] <= query_pos[:, None, None]
        )
        block_peak, block_total, block_out = block_terms(
            q_four, key_block, value_block, allowed_mask, score_scale
        )
        new_peak = jnp.maximum(run_peak, block_peak)
        old_factor = jnp.exp(run_peak - new_peak)
        new_factor = jnp.exp(block_peak - new_peak)
        new_total = run_total * old_factor + block_total * new_factor
        new_out = run_out * old_factor[..., None] + block_out * new_factor[..., None]
        return (new_peak, new_total, new_out)

    start_carry = (
        jnp.full((q_total, heads_local), NEG_FILL, jnp.float32),
        jnp.zeros((q_total, heads_local), jnp.float32),
        jnp.zeros((q_total, heads_local, head_width), jnp.float32),
    )
    block_order = jnp.arange(local_blocks, dtype=jnp.int32)
    local_peak, local_total, local_out = lax.fori_loop(
        0, local_blocks, partial(visit_block, block_order=block_order), start_carry
    )
    top_peak = lax.pmax(local_peak, "ctx")
    factor = jnp.exp(local_peak - top_peak)
    out_sum, total_sum = lax.psum((local_out * factor[..., None], local_total * factor), "ctx")
    attention = (
        (out_sum / total_sum[..., None])
        .reshape(q_total, heads_local * head_width)
        .astype(jnp.bfloat16)
    )
    return lax.psum_scatter(
        jnp.dot(attention, out_weight, preferred_element_type=jnp.float32),
        "head",
        scatter_dimension=0,
        tiled=True,
    ).astype(jnp.bfloat16)


def solution(mesh):
    return jax.shard_map(
        body,
        mesh=mesh,
        in_specs=(
            P("ctx", "head"),
            P("ctx", "head", None),
            P("ctx", "head", None),
            P("head", None),
            P("head", None),
            P("head", "ctx"),
        ),
        out_specs=P("head", "ctx"),
        check_vma=False,
    )
```

profile of v0, /device:TPU:0, one launch (start us, length us, event | category | flops | bytes accessed | tf_op | source)
XLA Modules:
  0.0 782.0 jit_solution(12740327105892136741)
XLA Ops:
  11.5 77.0 %all-gather.2.cloned.1.call-done = bf16[512,4096]{1,0:T(8,128)(2,1)} async-done(((bf16[32,4096]{1,0:T(8,128)(2,1)}), bf16[512,4096]{1,0:T(8,128)(2,1)}) %all-gather.2.cloned.1.call-update) | async-done | bytes 4194320 | tf_op jit(solution)/shard_map/all_gather | solution.py:43
  101.2 286.1 %while.20 = (s32[]{:T(128)}, f32[512,32]{0,1:T(8,128)S(1)}, f32[512,32]{0,1:T(8,128)S(1)}, f32[512,32,128]{0,2,1:T(8,128)}, s32[8]{0:T(128)S(1)}, /*index=5*/pre...) while((s32[]{:T(128)}, f32[512,32]{0,1:T(8,128)S(1)}, ...), condition=%wide.region_5.6_spmd.clone, body=%wide.region_2.5_spmd.clone.sunk | while | flops 1115882112 | bytes 98932640 | solution.py:89
  113.2 9.3 %fusion.30 = f32[4,128,512,8]{2,1,3,0:T(8,128)} fusion(bf16[128,4,128]{0,2,1:T(8,128)(2,1)S(1)} %copy.48, f32[4,128,512,8]{2,1,3,0:T(8,128)} %get-tuple-element.442, f32[512,4,8]{0,2,1:T(8,128)S(1)} %compare_select_fusion.2, pred[512,128]{0,1:T(8,128)(4,1)S(1)} %broadcast_compare_fusion.2, pred[512,4,8]{0,2,1:T(8,128)(4,1)S(1)} %and.85), kind=kOutput, calls=%fused_computation.14.clone.1 | convolution fusion | flops 547356672 | bytes 17055744 | tf_op jit(solution)/shard_map/while/body/eval_jaxpr/qgjk,kgd->qgjd/dot_general | solution.py:30
  125.2 9.6 %fusion.31 = f32[512,32,128]{0,2,1:T(8,128)} fusion(f32[4,128,512,8]{2,1,3,0:T(8,128)} %fusion.30, f32[512,32,128]{0,2,1:T(8,128)} %get-tuple-element.466, f32[512,32]{0,1:T(8,128)S(1)} %get-tuple-element.446, f32[512,32]{0,1:T(8,128)S(1)} %get-tuple-element.447, pred[]{:T(512)S(6)} %compare.3), kind=kLoop, calls=%fused_computation.6.clone.1 | loop fusion | flops 8388608 | bytes 25296896 | tf_op jit(solution)/shard_map/while/body/eval_jaxpr/add | solution.py:80
  139.2 7.5 fusion.28
  146.9 9.3 %fusion.30 = f32[4,128,512,8]{2,1,3,0:T(8,128)} fusion(bf16[128,4,128]{0,2,1:T(8,128)(2,1)S(1)} %copy.48, f32[4,128,512,8]{2,1,3,0:T(8,128)} %get-tuple-element.442, f32[512,4,8]{0,2,1:T(8,128)S(1)} %compare_select_fusion.2, pred[512,128]{0,1:T(8,128)(4,1)S(1)} %broadcast_compare_fusion.2, pred[512,4,8]{0,2,1:T(8,128)(4,1)S(1)} %and.85), kind=kOutput, calls=%fused_computation.14.clone.1 | convolution fusion | flops 547356672 | bytes 17055744 | tf_op jit(solution)/shard_map/while/body/eval_jaxpr/qgjk,kgd->qgjd/dot_general | solution.py:30
  158.9 12.0 %fusion.31 = f32[512,32,128]{0,2,1:T(8,128)} fusion(f32[4,128,512,8]{2,1,3,0:T(8,128)} %fusion.30, f32[512,32,128]{0,2,1:T(8,128)} %get-tuple-element.466, f32[512,32]{0,1:T(8,128)S(1)} %get-tuple-element.446, f32[512,32]{0,1:T(8,128)S(1)} %get-tuple-element.447, pred[]{:T(512)S(6)} %compare.3), kind=kLoop, calls=%fused_computation.6.clone.1 | loop fusion | flops 8388608 | bytes 25296896 | tf_op jit(solution)/shard_map/while/body/eval_jaxpr/add | solution.py:80
  175.3 7.5 fusion.28
  182.9 9.3 %fusion.30 = f32[4,128,512,8]{2,1,3,0:T(8,128)} fusion(bf16[128,4,128]{0,2,1:T(8,128)(2,1)S(1)} %copy.48, f32[4,128,512,8]{2,1,3,0:T(8,128)} %get-tuple-element.442, f32[512,4,8]{0,2,1:T(8,128)S(1)} %compare_select_fusion.2, pred[512,128]{0,1:T(8,128)(4,1)S(1)} %broadcast_compare_fusion.2, pred[512,4,8]{0,2,1:T(8,128)(4,1)S(1)} %and.85), kind=kOutput, calls=%fused_computation.14.clone.1 | convolution fusion | flops 547356672 | bytes 17055744 | tf_op jit(solution)/shard_map/while/body/eval_jaxpr/qgjk,kgd->qgjd/dot_general | solution.py:30
  194.9 12.0 %fusion.31 = f32[512,32,128]{0,2,1:T(8,128)} fusion(f32[4,128,512,8]{2,1,3,0:T(8,128)} %fusion.30, f32[512,32,128]{0,2,1:T(8,128)} %get-tuple-element.466, f32[512,32]{0,1:T(8,128)S(1)} %get-tuple-element.446, f32[512,32]{0,1:T(8,128)S(1)} %get-tuple-element.447, pred[]{:T(512)S(6)} %compare.3), kind=kLoop, calls=%fused_computation.6.clone.1 | loop fusion | flops 8388608 | bytes 25296896 | tf_op jit(solution)/shard_map/while/body/eval_jaxpr/add | solution.py:80
  219.0 9.3 %fusion.30 = f32[4,128,512,8]{2,1,3,0:T(8,128)} fusion(bf16[128,4,128]{0,2,1:T(8,128)(2,1)S(1)} %copy.48, f32[4,128,512,8]{2,1,3,0:T(8,128)} %get-tuple-element.442, f32[512,4,8]{0,2,1:T(8,128)S(1)} %compare_select_fusion.2, pred[512,128]{0,1:T(8,128)(4,1)S(1)} %broadcast_compare_fusion.2, pred[512,4,8]{0,2,1:T(8,128)(4,1)S(1)} %and.85), kind=kOutput, calls=%fused_computation.14.clone.1 | convolution fusion | flops 547356672 | bytes 17055744 | tf_op jit(solution)/shard_map/while/body/eval_jaxpr/qgjk,kgd->qgjd/dot_general | solution.py:30
  231.0 12.0 %fusion.31 = f32[512,32,128]{0,2,1:T(8,128)} fusion(f32[4,128,512,8]{2,1,3,0:T(8,128)} %fusion.30, f32[512,32,128]{0,2,1:T(8,128)} %get-tuple-element.466, f32[512,32]{0,1:T(8,128)S(1)} %get-tuple-element.446, f32[512,32]{0,1:T(8,128)S(1)} %get-tuple-element.447, pred[]{:T(512)S(6)} %compare.3), kind=kLoop, calls=%fused_computation.6.clone.1 | loop fusion | flops 8388608 | bytes 25296896 | tf_op jit(solution)/shard_map/while/body/eval_jaxpr/add | solution.py:80
  255.0 9.3 %fusion.30 = f32[4,128,512,8]{2,1,3,0:T(8,128)} fusion(bf16[128,4,128]{0,2,1:T(8,128)(2,1)S(1)} %copy.48, f32[4,128,512,8]{2,1,3,0:T(8,128)} %get-tuple-element.442, f32[512,4,8]{0,2,1:T(8,128)S(1)} %compare_select_fusion.2, pred[512,128]{0,1:T(8,128)(4,1)S(1)} %broadcast_compare_fusion.2, pred[512,4,8]{0,2,1:T(8,128)(4,1)S(1)} %and.85), kind=kOutput, calls=%fused_computation.14.clone.1 | convolution fusion | flops 547356672 | bytes 17055744 | tf_op jit(solution)/shard_map/while/body/eval_jaxpr/qgjk,kgd->qgjd/dot_general | solution.py:30
  267.1 12.0 %fusion.31 = f32[512,32,128]{0,2,1:T(8,128)} fusion(f32[4,128,512,8]{2,1,3,0:T(8,128)} %fusion.30, f32[512,32,128]{0,2,1:T(8,128)} %get-tuple-element.466, f32[512,32]{0,1:T(8,128)S(1)} %get-tuple-element.446, f32[512,32]{0,1:T(8,128)S(1)} %get-tuple-element.447, pred[]{:T(512)S(6)} %compare.3), kind=kLoop, calls=%fused_computation.6.clone.1 | loop fusion | flops 8388608 | bytes 25296896 | tf_op jit(solution)/shard_map/while/body/eval_jaxpr/add | solution.py:80
  291.1 9.3 %fusion.30 = f32[4,128,512,8]{2,1,3,0:T(8,128)} fusion(bf16[128,4,128]{0,2,1:T(8,128)(2,1)S(1)} %copy.48, f32[4,128,512,8]{2,1,3,0:T(8,128)} %get-tuple-element.442, f32[512,4,8]{0,2,1:T(8,128)S(1)} %compare_select_fusion.2, pred[512,128]{0,1:T(8,128)(4,1)S(1)} %broadcast_compare_fusion.2, pred[512,4,8]{0,2,1:T(8,128)(4,1)S(1)} %and.85), kind=kOutput, calls=%fused_computation.14.clone.1 | convolution fusion | flops 547356672 | bytes 17055744 | tf_op jit(solution)/shard_map/while/body/eval_jaxpr/qgjk,kgd->qgjd/dot_general | solution.py:30
  303.1 12.0 %fusion.31 = f32[512,32,128]{0,2,1:T(8,128)} fusion(f32[4,128,512,8]{2,1,3,0:T(8,128)} %fusion.30, f32[512,32,128]{0,2,1:T(8,128)} %get-tuple-element.466, f32[512,32]{0,1:T(8,128)S(1)} %get-tuple-element.446, f32[512,32]{0,1:T(8,128)S(1)} %get-tuple-element.447, pred[]{:T(512)S(6)} %compare.3), kind=kLoop, calls=%fused_computation.6.clone.1 | loop fusion | flops 8388608 | bytes 25296896 | tf_op jit(solution)/shard_map/while/body/eval_jaxpr/add | solution.py:80
  327.2 9.3 %fusion.30 = f32[4,128,512,8]{2,1,3,0:T(8,128)} fusion(bf16[128,4,128]{0,2,1:T(8,128)(2,1)S(1)} %copy.48, f32[4,128,512,8]{2,1,3,0:T(8,128)} %get-tuple-element.442, f32[512,4,8]{0,2,1:T(8,128)S(1)} %compare_select_fusion.2, pred[512,128]{0,1:T(8,128)(4,1)S(1)} %broadcast_compare_fusion.2, pred[512,4,8]{0,2,1:T(8,128)(4,1)S(1)} %and.85), kind=kOutput, calls=%fused_computation.14.clone.1 | convolution fusion | flops 547356672 | bytes 17055744 | tf_op jit(solution)/shard_map/while/body/eval_jaxpr/qgjk,kgd->qgjd/dot_general | solution.py:30
  339.2 12.0 %fusion.31 = f32[512,32,128]{0,2,1:T(8,128)} fusion(f32[4,128,512,8]{2,1,3,0:T(8,128)} %fusion.30, f32[512,32,128]{0,2,1:T(8,128)} %get-tuple-element.466, f32[512,32]{0,1:T(8,128)S(1)} %get-tuple-element.446, f32[512,32]{0,1:T(8,128)S(1)} %get-tuple-element.447, pred[]{:T(512)S(6)} %compare.3), kind=kLoop, calls=%fused_computation.6.clone.1 | loop fusion | flops 8388608 | bytes 25296896 | tf_op jit(solution)/shard_map/while/body/eval_jaxpr/add | solution.py:80
  363.2 9.3 %fusion.30 = f32[4,128,512,8]{2,1,3,0:T(8,128)} fusion(bf16[128,4,128]{0,2,1:T(8,128)(2,1)S(1)} %copy.48, f32[4,128,512,8]{2,1,3,0:T(8,128)} %get-tuple-element.442, f32[512,4,8]{0,2,1:T(8,128)S(1)} %compare_select_fusion.2, pred[512,128]{0,1:T(8,128)(4,1)S(1)} %broadcast_compare_fusion.2, pred[512,4,8]{0,2,1:T(8,128)(4,1)S(1)} %and.85), kind=kOutput, calls=%fused_computation.14.clone.1 | convolution fusion | flops 547356672 | bytes 17055744 | tf_op jit(solution)/shard_map/while/body/eval_jaxpr/qgjk,kgd->qgjd/dot_general | solution.py:30
  375.2 12.0 %fusion.31 = f32[512,32,128]{0,2,1:T(8,128)} fusion(f32[4,128,512,8]{2,1,3,0:T(8,128)} %fusion.30, f32[512,32,128]{0,2,1:T(8,128)} %get-tuple-element.466, f32[512,32]{0,1:T(8,128)S(1)} %get-tuple-element.446, f32[512,32]{0,1:T(8,128)S(1)} %get-tuple-element.447, pred[]{:T(512)S(6)} %compare.3), kind=kLoop, calls=%fused_computation.6.clone.1 | loop fusion | flops 8388608 | bytes 25296896 | tf_op jit(solution)/shard_map/while/body/eval_jaxpr/add | solution.py:80
  388.1 102.2 %all-reduce.4.cloned.1.call-done = f32[512,32]{0,1:T(8,128)} async-done(((f32[512,32]{0,1:T(8,128)}), f32[512,32]{0,1:T(8,128)}) %all-reduce.4.cloned.1.call-update) | async-done | bytes 65552 | tf_op jit(solution)/shard_map/pmax | solution.py:92
  491.8 8.3 %broadcast_multiply_fusion = f32[512,32,128]{0,2,1:T(8,128)} fusion(f32[512,32,128]{0,2,1:T(8,128)} %get-tuple-element.261, f32[512,32]{0,1:T(8,128)S(1)} %get-tuple-element.366), kind=kLoop, calls=%fused_computation.30 | loop fusion | flops 2097152 | bytes 16842752 | tf_op jit(solution)/shard_map/mul | solution.py:94
  500.2 257.8 %all-reduce.6.cloned.1.call-done = (f32[512,32,128]{0,2,1:T(8,128)}, f32[512,32]{0,1:T(8,128)}) async-done(((f32[512,32,128]{0,2,1:T(8,128)}, f32[512,32]{0,1:T(8,128)}), (f32[512,32,128]{0,2,1:T(8,128)}, f32[512,32]{0,1:T(8,128)})) %all-reduce.6.cloned.1.call-update) | async-done | bytes 8454160 | tf_op jit(solution)/shard_map/psum | solution.py:94
  766.2 7.6 reduce-scatter.2.cloned.1.call-done
  (156 shorter events, 113.5 us)
Async XLA Ops:
  6.5 81.9 %all-gather.2.cloned.1.call-start = ((), (), s32[]{:S(2)}) async-start(), calls=%async_computation.1 | async-start | bytes 4456448 | tf_op jit(solution)/shard_map/all_gather | solution.py:43
  7.3 483.0 %all-reduce.4.cloned.1.call-start = ((), (), s32[]{:S(2)}) async-start(), calls=%async_computation.2 | async-start | bytes 131072 | tf_op jit(solution)/shard_map/pmax | solution.py:92
  113.2 9.3 %copy-start = (f32[4,128,512,8]{2,1,3,0:T(8,128)S(1)}, f32[4,128,512,8]{2,1,3,0:T(8,128)}, u32[]{:S(2)}) copy-start(f32[4,128,512,8]{2,1,3,0:T(8,128)} %get-tuple-element.442) | copy-start | bytes 25165828 | tf_op jit(solution)/shard_map/while
  146.9 9.3 %copy-start = (f32[4,128,512,8]{2,1,3,0:T(8,128)S(1)}, f32[4,128,512,8]{2,1,3,0:T(8,128)}, u32[]{:S(2)}) copy-start(f32[4,128,512,8]{2,1,3,0:T(8,128)} %get-tuple-element.442) | copy-start | bytes 25165828 | tf_op jit(solution)/shard_map/while
  182.9 9.3 %copy-start = (f32[4,128,512,8]{2,1,3,0:T(8,128)S(1)}, f32[4,128,512,8]{2,1,3,0:T(8,128)}, u32[]{:S(2)}) copy-start(f32[4,128,512,8]{2,1,3,0:T(8,128)} %get-tuple-element.442) | copy-start | bytes 25165828 | tf_op jit(solution)/shard_map/while
  219.0 9.3 %copy-start = (f32[4,128,512,8]{2,1,3,0:T(8,128)S(1)}, f32[4,128,512,8]{2,1,3,0:T(8,128)}, u32[]{:S(2)}) copy-start(f32[4,128,512,8]{2,1,3,0:T(8,128)} %get-tuple-element.442) | copy-start | bytes 25165828 | tf_op jit(solution)/shard_map/while
  255.0 9.3 %copy-start = (f32[4,128,512,8]{2,1,3,0:T(8,128)S(1)}, f32[4,128,512,8]{2,1,3,0:T(8,128)}, u32[]{:S(2)}) copy-start(f32[4,128,512,8]{2,1,3,0:T(8,128)} %get-tuple-element.442) | copy-start | bytes 25165828 | tf_op jit(solution)/shard_map/while
  291.1 9.3 %copy-start = (f32[4,128,512,8]{2,1,3,0:T(8,128)S(1)}, f32[4,128,512,8]{2,1,3,0:T(8,128)}, u32[]{:S(2)}) copy-start(f32[4,128,512,8]{2,1,3,0:T(8,128)} %get-tuple-element.442) | copy-start | bytes 25165828 | tf_op jit(solution)/shard_map/while
  327.1 9.3 %copy-start = (f32[4,128,512,8]{2,1,3,0:T(8,128)S(1)}, f32[4,128,512,8]{2,1,3,0:T(8,128)}, u32[]{:S(2)}) copy-start(f32[4,128,512,8]{2,1,3,0:T(8,128)} %get-tuple-element.442) | copy-start | bytes 25165828 | tf_op jit(solution)/shard_map/while
  363.2 9.3 %copy-start = (f32[4,128,512,8]{2,1,3,0:T(8,128)S(1)}, f32[4,128,512,8]{2,1,3,0:T(8,128)}, u32[]{:S(2)}) copy-start(f32[4,128,512,8]{2,1,3,0:T(8,128)} %get-tuple-element.442) | copy-start | bytes 25165828 | tf_op jit(solution)/shard_map/while
  387.3 0.6 copy-start.2
  387.9 370.0 %all-reduce.6.cloned.1.call-start = ((), (), s32[]{:S(2)}) async-start(), calls=%async_computation.4 | async-start | bytes 16908288 | tf_op jit(solution)/shard_map/psum | solution.py:94
  500.1 273.6 %reduce-scatter.2.cloned.1.call-start = ((), (), s32[]{:S(2)}) async-start(), calls=%async_computation.3 | async-start | bytes 1572864 | tf_op jit(solution)/shard_map/reduce_scatter | solution.py:100
  757.9 4.9 copy-start.1
Sparse Core Ops, SparseCore 0:
  10.1 78.3 all-gather.1
  388.0 102.2 all-reduce.3
  500.2 257.6 all-reduce.5
  766.3 7.4 reduce-scatter.1
where the time goes:
time: 783 us; the launch traced here: 782 us
  waiting for transfers between devices  445 us (57%)
  matrix products  138 us (18%)
  other arithmetic  136 us (17%)
  local copies, waits for them, and re-layouts  29.7 us (4%)
  loops' own time  19.2 us (2%)
  between operations  13.2 us (2%)
    psum x1, waiting for transfers between devices, body(): lax.psum((local_out * factor[..., None], local_total * factor), 'ctx')  258 us
    pmax x1, waiting for transfers between devices, body(): top_peak = lax.pmax(local_peak, 'ctx')  102 us
    add x8, other arithmetic, visit_block(): run_out * old_factor[..., None] + block_out * new_factor[..., None]  93.7 us
    all_gather x1, waiting for transfers between devices, body(): q_whole = lax.all_gather(queries, 'ctx', axis=0, tiled=True)  77 us
    dot_general x8, matrix products, block_terms(): jnp.einsum('qgjk,kgd->qgjd', weights_four, value_block, preferred_element...  74.7 us
    dot_general x8, matrix products, block_terms(): jnp.einsum('qgjd,kgd->qgjk', q_four, key_block, preferred_element_type=jn...  60 us
    reduce_sum x8, other arithmetic, block_terms(): block_total = jnp.sum(weights.astype(jnp.float32), axis=-1)  20.9 us
    another operation x1, loops' own time, body(): lax.fori_loop(0, local_blocks, partial(visit_block, block_order=block_ord...  19.2 us
  transfers between devices with their start and end apart: 4, of which 4 were waited for; matrix products, arithmetic and copies ran while one was open for 1% of the time, Pallas kernels for 0%

commit v1 on v0

v1 whole, which is shorter than its diff:
```python
from functools import partial
import math

import jax
import jax.numpy as jnp
from jax import lax
from jax.experimental import pallas as pl
from jax.experimental.pallas import tpu as pltpu
from jax.sharding import PartitionSpec as P

BLOCK = 128
NEG_FILL = -1e30
CHUNK = 4
PAIR = 2
ONES_ROWS = 16


def transpose_values_kernel(v_ref, vt_ref):
    blocks = vt_ref.shape[0] - 1
    width = v_ref.shape[1]
    rows = vt_ref.shape[1]
    for i in range(blocks):
        vt_ref[i, 0:width, :] = v_ref[i * BLOCK : (i + 1) * BLOCK, :].T
        vt_ref[i, width:rows, :] = jnp.ones((rows - width, BLOCK), vt_ref.dtype)
    vt_ref[blocks] = jnp.zeros((rows, BLOCK), vt_ref.dtype)


def transpose_values(values):
    keys, width = values.shape
    return pl.pallas_call(
        transpose_values_kernel,
        out_shape=jax.ShapeDtypeStruct((keys // BLOCK + 1, width + ONES_ROWS, BLOCK), values.dtype),
        name="transpose_values",
    )(values)


def attention_kernel(
    turn_ref, count_ref, diag_ref, klist_ref, vlist_ref, q_ref, k_ref, vt_ref, o_ref, lse_ref, m_sc, acc_sc,
    *, scale2, list_len,
):
    heads = o_ref.shape[0]
    width = o_ref.shape[1]
    turn = turn_ref[0]
    diag = diag_ref[turn]

    def scores_of(keys, h):
        q = q_ref[:, h * width : (h + 1) * width]
        return lax.dot_general(keys, q, (((1,), (1,)), ((), ())), preferred_element_type=jnp.float32)

    m_sc[...] = jnp.full(m_sc.shape, NEG_FILL, jnp.float32)
    acc_sc[...] = jnp.zeros(acc_sc.shape, jnp.float32)

    @pl.when(diag >= 0)
    def _():
        keys = k_ref[pl.ds(pl.multiple_of(diag * BLOCK, BLOCK), BLOCK), :]
        values = vt_ref[diag]
        causal = lax.broadcasted_iota(jnp.int32, (BLOCK, BLOCK), 0) <= lax.broadcasted_iota(
            jnp.int32, (BLOCK, BLOCK), 1
        )
        for h in range(heads):
            s = jnp.where(causal, scores_of(keys, h) * scale2, NEG_FILL)
            m = jnp.max(s, axis=0, keepdims=True)
            p = jnp.exp2(s - m).astype(jnp.bfloat16)
            m_sc[h : h + 1, :] = m
            acc_sc[h] = jnp.dot(values, p, preferred_element_type=jnp.float32)

    for h0 in range(0, heads, PAIR):
        group = range(h0, min(h0 + PAIR, heads))
        counts = [count_ref[turn * heads + h] for h in group]
        most = counts[0]
        for c in counts[1:]:
            most = jnp.maximum(most, c)

        def visit(t, carry, group=group, counts=counts):
            out = []
            for i, h in enumerate(group):
                m, acc = carry[i]
                base = (turn * heads + h) * list_len + t * CHUNK
                keys = jnp.concatenate(
                    [
                        k_ref[pl.ds(pl.multiple_of(klist_ref[base + u] * BLOCK, BLOCK), BLOCK), :]
                        for u in range(CHUNK)
                    ],
                    axis=0,
                )
                values = jnp.concatenate([vt_ref[vlist_ref[base + u]] for u in range(CHUNK)], axis=1)
                s = scores_of(keys, h)
                top = jnp.max(s, axis=0, keepdims=True) * scale2
                m_new = jnp.maximum(m, jnp.where(t * CHUNK < counts[i], top, NEG_FILL))
                p = jnp.exp2(s * scale2 - jnp.maximum(m_new, top)).astype(jnp.bfloat16)
                acc = acc * jnp.exp2(m - m_new) + jnp.dot(values, p, preferred_element_type=jnp.float32)
                out.append((m_new, acc))
            return tuple(out)

        start = tuple((m_sc[h : h + 1, :], acc_sc[h]) for h in group)
        done = lax.fori_loop(0, (most + CHUNK - 1) // CHUNK, visit, start)
        for i, h in enumerate(group):
            m, acc = done[i]
            total = acc[width : width + 1, :]
            seen = total > 0.0
            safe = jnp.where(seen, total, 1.0)
            o_ref[h] = (acc[0:width, :] / safe).astype(o_ref.dtype)
            lse_ref[h : h + 1, :] = jnp.where(seen, m + jnp.log2(safe), NEG_FILL)


def block_attention(turn, meta, q, keys, vt):
    count, diag, klist, vlist = meta
    turns = diag.shape[0]
    heads = count.shape[0] // turns
    width = keys.shape[1]
    smem = pl.BlockSpec(memory_space=pltpu.SMEM)
    vmem = pl.BlockSpec(memory_space=pltpu.VMEM)
    return pl.pallas_call(
        partial(
            attention_kernel,
            scale2=float(width) ** -0.5 * math.log2(math.e),
            list_len=klist.shape[0] // count.shape[0],
        ),
        out_shape=(
            jax.ShapeDtypeStruct((heads, width, BLOCK), jnp.bfloat16),
            jax.ShapeDtypeStruct((heads, BLOCK), jnp.float32),
        ),
        in_specs=[smem] * 5 + [vmem] * 3,
        out_specs=(vmem, vmem),
        scratch_shapes=[
            pltpu.VMEM((heads, BLOCK), jnp.float32),
            pltpu.VMEM((heads, width + ONES_ROWS, BLOCK), jnp.float32),
        ],
        name="block_attention",
    )(jnp.full((1,), turn, jnp.int32), count, diag, klist, vlist, q, keys, vt)


def combine_kernel(*refs):
    parts = (len(refs) - 1) // 2
    outs, lses, att_ref = refs[:parts], refs[parts : 2 * parts], refs[-1]
    heads, width = outs[0].shape[0], outs[0].shape[1]
    lse = [ref[...] for ref in lses]
    top = lse[0]
    for x in lse[1:]:
        top = jnp.maximum(top, x)
    weight = [jnp.exp2(x - top) for x in lse]
    total = weight[0]
    for x in weight[1:]:
        total = total + x
    inverse = 1.0 / total
    weight = [x * inverse for x in weight]
    for h in range(heads):
        mixed = outs[0][h].astype(jnp.float32) * weight[0][h : h + 1, :]
        for ref, x in zip(outs[1:], weight[1:]):
            mixed = mixed + ref[h].astype(jnp.float32) * x[h : h + 1, :]
        att_ref[:, h * width : (h + 1) * width] = mixed.T.astype(att_ref.dtype)


def combine(outs, lses):
    heads, width, rows = outs[0].shape
    return pl.pallas_call(
        combine_kernel,
        out_shape=jax.ShapeDtypeStruct((rows, heads * width), jnp.bfloat16),
        name="combine",
    )(*outs, *lses)


def block_lists(vertical, slash, query_blocks, first_block, local_blocks):
    ids = first_block + jnp.arange(local_blocks, dtype=jnp.int32)
    offsets = query_blocks[:, None] - ids[None, :]
    vertical_hit = jnp.any(vertical[:, :, None] == ids[None, None, :], axis=1)
    slash_hit = jnp.any(slash[None, :, :, None] == offsets[:, None, None, :], axis=2)
    picked = (vertical_hit[None] | slash_hit) & (offsets > 0)[:, None, :]
    picked = picked.astype(jnp.int32)
    order = jnp.arange(local_blocks, dtype=jnp.int32)
    rank = jnp.sum(picked[:, :, None, :] * (order[None, :] < order[:, None]), axis=3)
    count = jnp.sum(picked, axis=2)
    list_len = -(-local_blocks // CHUNK) * CHUNK
    slot = jnp.arange(list_len, dtype=jnp.int32)
    wanted = jnp.where(slot[None, None, :] < count[:, :, None], slot[None, None, :], 0)
    match = picked[:, :, None, :] * (rank[:, :, None, :] == wanted[:, :, :, None])
    klist = jnp.sum(match * order, axis=3)
    vlist = jnp.where(slot[None, None, :] < count[:, :, None], klist, local_blocks)
    diag = query_blocks - first_block
    diag = jnp.where((diag >= 0) & (diag < local_blocks), diag, -1)
    return count.reshape(-1), diag, klist.reshape(-1), vlist.reshape(-1)


def plane_body(queries, cache_keys, cache_values, vertical_blocks, slash_offsets, out_weight):
    ctx_count = lax.axis_size("ctx")
    core_count = lax.axis_size("head")
    place = lax.axis_index("ctx")
    local_len, plane, width = cache_keys.shape
    lines = ctx_count // plane
    line, mine = place // plane, place % plane
    q_rows = queries.shape[0]
    heads = vertical_blocks.shape[0] // plane
    feats = heads * width
    columns = out_weight.shape[1]
    span = plane * local_len
    local_blocks = span // BLOCK
    all_blocks = local_blocks * lines
    planes = [[a * plane + b for b in range(plane)] for a in range(lines)]
    swap = partial(
        lax.all_to_all, axis_name="ctx", split_axis=0, concat_axis=0, axis_index_groups=planes, tiled=True
    )

    def along(x, step):
        pairs = [
            (a * plane + b, ((a + step) % lines) * plane + b) for a in range(lines) for b in range(plane)
        ]
        return lax.ppermute(x, "ctx", pairs)

    q_own = swap(jnp.transpose(queries.reshape(q_rows, plane, feats), (1, 0, 2))).reshape(plane * q_rows, feats)
    q_parts = [q_own] + [along(q_own, -k) for k in range(1, lines)]
    keys = swap(jnp.transpose(cache_keys, (1, 0, 2))).reshape(span, width)
    values = swap(jnp.transpose(cache_values, (1, 0, 2))).reshape(span, width)
    keys, values, weight = lax.optimization_barrier((keys, values, out_weight))
    weight = swap(weight.reshape(plane, feats, columns))
    vt = transpose_values(values)

    turns = (line + jnp.arange(lines, dtype=jnp.int32)) % lines
    meta = block_lists(
        lax.dynamic_slice_in_dim(vertical_blocks, mine * heads, heads, 0),
        lax.dynamic_slice_in_dim(slash_offsets, mine * heads, heads, 0),
        all_blocks - lines + turns,
        line * local_blocks,
        local_blocks,
    )
    outs, lses = [None] * lines, [None] * lines
    for k in list(range(1, lines)) + [0]:
        o, l = block_attention(k, meta, q_parts[k], keys, vt)
        outs[k], lses[k] = (along(o, k), along(l, k)) if k else (o, l)
    att = combine(outs, lses)
    full = jnp.zeros((lines, BLOCK, feats), jnp.bfloat16)
    for k in range(lines):
        part = along(att, -k) if k else att
        full = lax.dynamic_update_slice_in_dim(full, part[None], turns[k], 0)

    core = lax.axis_index("head")
    full = full.reshape(core_count, lines * BLOCK // core_count, feats)
    rows = full.shape[1]

    def project(which):
        part = lax.dynamic_index_in_dim(full, which, 0, keepdims=False)
        return jnp.stack(
            [jnp.dot(part, weight[j], preferred_element_type=jnp.float32) for j in range(plane)]
        )

    sums = None
    for step in range(1, core_count):
        away = project((core + step) % core_count).astype(jnp.bfloat16)
        got = lax.ppermute(away, "head", [(a, (a + step) % core_count) for a in range(core_count)])
        got = got.astype(jnp.float32)
        sums = got if sums is None else sums + got
    own = project(core)
    sums = own if sums is None else sums + own
    got = swap(sums.astype(jnp.bfloat16))
    return jnp.sum(got.astype(jnp.float32), axis=0).astype(jnp.bfloat16)


def general_body(queries, cache_keys, cache_values, vertical_blocks, slash_offsets, out_weight):
    ctx_count = lax.axis_size("ctx")
    place = lax.axis_index("ctx")
    local_len, kv_local, width = cache_keys.shape
    heads = vertical_blocks.shape[0] // kv_local
    feats = heads * width
    q_whole = lax.all_gather(queries, "ctx", axis=0, tiled=True)
    q_blocks = q_whole.shape[0] // BLOCK
    local_blocks = local_len // BLOCK
    query_blocks = local_blocks * ctx_count - q_blocks + jnp.arange(q_blocks, dtype=jnp.int32)
    attention = []
    for g in range(kv_local):
        meta = block_lists(
            vertical_blocks[g * heads : (g + 1) * heads],
            slash_offsets[g * heads : (g + 1) * heads],
            query_blocks,
            place * local_blocks,
            local_blocks,
        )
        vt = transpose_values(cache_values[:, g, :])
        outs, lses = [], []
        for b in range(q_blocks):
            q = q_whole[b * BLOCK : (b + 1) * BLOCK, g * feats : (g + 1) * feats]
            o, l = block_attention(b, meta, q, cache_keys[:, g, :], vt)
            outs.append(o)
            lses.append(l)
        out, lse = jnp.stack(outs), jnp.stack(lses)
        factor = jnp.exp2(lse - lax.pmax(lse, "ctx"))
        out, total = lax.psum((out.astype(jnp.float32) * factor[:, :, None, :], factor), "ctx")
        out = (out / total[:, :, None, :]).astype(jnp.bfloat16)
        attention.append(jnp.transpose(out, (0, 3, 1, 2)).reshape(q_blocks * BLOCK, feats))
    return lax.psum_scatter(
        jnp.dot(jnp.concatenate(attention, axis=1), out_weight, preferred_element_type=jnp.float32),
        "head",
        scatter_dimension=0,
        tiled=True,
    ).astype(jnp.bfloat16)


def body(queries, cache_keys, cache_values, vertical_blocks, slash_offsets, out_weight):
    ctx_count = lax.axis_size("ctx")
    lines = queries.shape[0] * ctx_count // BLOCK
    fits = cache_keys.shape[1] * lines == ctx_count and lines % lax.axis_size("head") == 0
    chosen = plane_body if fits else general_body
    return chosen(queries, cache_keys, cache_values, vertical_blocks, slash_offsets, out_weight)


def solution(mesh):
    return jax.shard_map(
        body,
        mesh=mesh,
        in_specs=(
            P("ctx", "head"),
            P("ctx", "head", None),
            P("ctx", "head", None),
            P("head", None),
            P("head", None),
            P("head", "ctx"),
        ),
        out_specs=P("head", "ctx"),
        check_vma=False,
    )
```

time: 783 us -> 208 us (0.27)
  waiting for transfers between devices: 445 us -> 47.1 us
  other arithmetic: 136 us -> 5.22 us
  matrix products: 138 us -> 13.3 us
  starting transfers between devices: 0.3 us -> 68.8 us
  Pallas kernels: 0 us -> 37 us
  local copies, waits for them, and re-layouts: 29.7 us -> 10.1 us
  loops' own time: 19.2 us -> 0 us
  blocking collectives: 0 us -> 17.5 us
    psum x1 -> x0, waiting for transfers between devices: 258 us -> none  [body(): lax.psum((local_out * factor[..., None], local_total * factor), 'ctx')]
    dot_general x17 -> x8, matrix products: 138 us -> 13.3 us  [project(): jnp.dot(part, weight[j], preferred_element_type=jnp.float32)]
    pmax x1 -> x0, waiting for transfers between devices: 102 us -> none  [body(): top_peak = lax.pmax(local_peak, 'ctx')]
    add x34 -> x1, other arithmetic: 94.3 us -> 0.01 us  [block_lists(): ids = first_block + jnp.arange(local_blocks, dtype=jnp.int32)]
    all_gather x1 -> x0, waiting for transfers between devices: 77 us -> none  [body(): q_whole = lax.all_gather(queries, 'ctx', axis=0, tiled=True)]
    ppermute x0 -> x13, starting transfers between devices: none -> 51.8 us  [the longest x12 51.7 us: along(): return lax.ppermute(x, 'ctx', pairs)]
    pallas_call x0 -> x6, Pallas kernels: none -> 37 us  [the longest x4 32.2 us: block_attention(): pl.pallas_call(partial(attention_kernel, scale2=float(width) ** (-0.5) *...]
    all_to_all x0 -> x4, waiting for transfers between devices: none -> 29.8 us  [the longest x1 12.5 us: plane_body(): keys = swap(jnp.transpose(cache_keys, (1, 0, 2))).reshape(span, width)]
  transfers between devices with their start and end apart: 4 -> 17, of which waited for: 4 -> 6; matrix products, arithmetic and copies ran while one was open for 1% -> 7% of each run, Pallas kernels for 0% -> 18%
where the time goes in v1:
time: 208 us; the launch traced here: 207 us
  starting transfers between devices  68.8 us (33%)
  waiting for transfers between devices  47.1 us (23%)
  Pallas kernels  37 us (18%)
  blocking collectives  17.5 us (8%)
  matrix products  13.3 us (6%)
  local copies, waits for them, and re-layouts  10.1 us (5%)
  between operations  7.92 us (4%)
  other arithmetic  5.22 us (3%)
    ppermute x12, starting transfers between devices, along(): return lax.ppermute(x, 'ctx', pairs)  51.7 us
    pallas_call x4, Pallas kernels, block_attention(): pl.pallas_call(partial(attention_kernel, scale2=float(width) ** (-0.5) *...  32.2 us
    all_to_all x1, blocking collectives, plane_body(): got = swap(sums.astype(jnp.bfloat16))  17.5 us
    ppermute x12, waiting for transfers between devices, along(): return lax.ppermute(x, 'ctx', pairs)  17.3 us
    dot_general x8, matrix products, project(): jnp.dot(part, weight[j], preferred_element_type=jnp.float32)  13.3 us
    all_to_all x1, waiting for transfers between devices, plane_body(): keys = swap(jnp.transpose(cache_keys, (1, 0, 2))).reshape(span, width)  12.5 us
    all_to_all x1, waiting for transfers between devices, plane_body(): values = swap(jnp.transpose(cache_values, (1, 0, 2))).reshape(span, width)  12.1 us
    unnamed x38, local copies, waits for them, and re-layouts  6.52 us
  transfers between devices with their start and end apart: 17, of which 6 were waited for; matrix products, arithmetic and copies ran while one was open for 7% of the time, Pallas kernels for 18%

profile of v1, /device:TPU:0, one launch (start us, length us, event | category | flops | bytes accessed | tf_op | source)
XLA Modules:
  0.0 206.9 jit_solution(3090474014900016516)
XLA Ops:
  0.0 2.4 %copy.24 = bf16[1024,4,128]{2,0,1:T(8,128)(2,1)} copy(bf16[1024,4,128]{2,1,0:T(4,128)(2,1)} %param.7) | data formatting | bytes 2097152 | tf_op args[1]
  2.4 5.2 %all-to-all-start.1 = ((bf16[4,1024,128]{2,1,0:T(8,128)(2,1)}), bf16[4,1024,128]{2,1,0:T(8,128)(2,1)S(1)}, u32[]{:S(2)}, u32[]{:S(2)}) async-start(bf16[4,1024,128]{2,1,0:T(8,128)(2,1)} %bitcast.77), calls=%async_computation.1 | async-start | bytes 2097152 | tf_op jit(solution)/shard_map/all_to_all | solution.py:211
  8.8 12.5 %all-to-all-done.1 = bf16[4,1024,128]{2,1,0:T(8,128)(2,1)S(1)} async-done(((bf16[4,1024,128]{2,1,0:T(8,128)(2,1)}), bf16[4,1024,128]{2,1,0:T(8,128)(2,1)S(1)}, u32[]{:S(2)}, u32[]{:S(2)}) %all-to-all-start.1) | async-done | bytes 1048608 | tf_op jit(solution)/shard_map/all_to_all | solution.py:211
  21.3 3.5 %all-to-all-start.2 = ((bf16[4,1024,128]{2,1,0:T(8,128)(2,1)}), bf16[4,1024,128]{2,1,0:T(8,128)(2,1)S(1)}, u32[]{:S(2)}, u32[]{:S(2)}) async-start(bf16[4,1024,128]{2,1,0:T(8,128)(2,1)} %bitcast.76), calls=%async_computation.2 | async-start | bytes 2097152 | tf_op jit(solution)/shard_map/all_to_all | solution.py:212
  25.8 12.1 %all-to-all-done.2 = bf16[4,1024,128]{2,1,0:T(8,128)(2,1)S(1)} async-done(((bf16[4,1024,128]{2,1,0:T(8,128)(2,1)}), bf16[4,1024,128]{2,1,0:T(8,128)(2,1)S(1)}, u32[]{:S(2)}, u32[]{:S(2)}) %all-to-all-start.2) | async-done | bytes 1048608 | tf_op jit(solution)/shard_map/all_to_all | solution.py:212
  37.9 3.4 %all-to-all-start = ((bf16[4,32,1024]{2,1,0:T(8,128)(2,1)}), bf16[4,32,1024]{2,1,0:T(8,128)(2,1)S(1)}, u32[]{:S(2)}, u32[]{:S(2)}) async-start(bf16[4,32,1024]{2,1,0:T(8,128)(2,1)} %bitcast.79), calls=%async_computation | async-start | bytes 524288 | tf_op jit(solution)/shard_map/all_to_all | solution.py:209
  41.4 5.3 %all-to-all-done = bf16[4,32,1024]{2,1,0:T(8,128)(2,1)S(1)} async-done(((bf16[4,32,1024]{2,1,0:T(8,128)(2,1)}), bf16[4,32,1024]{2,1,0:T(8,128)(2,1)S(1)}, u32[]{:S(2)}, u32[]{:S(2)}) %all-to-all-start) | async-done | bytes 262176 | tf_op jit(solution)/shard_map/all_to_all | solution.py:209
  46.7 4.9 %all-to-all-start.3 = ((bf16[4,1024,512]{2,1,0:T(8,128)(2,1)}), bf16[4,1024,512]{2,1,0:T(8,128)(2,1)}, u32[]{:S(2)}, u32[]{:S(2)}) async-start(bf16[4,1024,512]{2,1,0:T(8,128)(2,1)} %bitcast.84), calls=%async_computation.3 | async-start | bytes 8388608 | tf_op jit(solution)/shard_map/all_to_all | solution.py:214
  55.7 2.6 %collective-permute-start.2 = (bf16[128,1024]{1,0:T(8,128)(2,1)S(1)}, bf16[128,1024]{1,0:T(8,128)(2,1)S(1)}, u32[]{:S(2)}, u32[]{:S(2)}) collective-permute-start(bf16[128,1024]{1,0:T(8,128)(2,1)S(1)} %bitcast.87), channel_id=1, source_target_pairs={{0,16},{2,18},{4,20},{6,22},{8,24},{10,26},{12,28},{14,30},{16,0},... | collective-permute-start | bytes 786440 | tf_op jit(solution)/shard_map/ppermute | solution.py:207
  61.6 2.6 %transpose_values.1.vt_ref = bf16[33,144,128]{2,1,0:T(8,128)(2,1)} custom-call(bf16[4096,128]{1,0:T(8,128)(2,1)} %bitcast.85), custom_call_target="tpu_custom_call" | custom-call | tf_op jit(solution)/shard_map/transpose_values/pallas_call | solution.py:30
  65.8 8.0 %block_attention.7 = (bf16[8,128,128]{2,1,0:T(8,128)(2,1)}, f32[8,128]{1,0:T(8,128)}) custom-call(s32[1]{0:T(128)} %constant.84.clone.1.turn_ref, s32[32]{0:T(128)} %reshape.129.count_ref, s32[4]{0:T(128)} %and_select_fusion.diag_ref, s32[1024]{0:T(1024)} %copy-done.12, s32[1024]{0:T(1024)} %broadcast_select_fusion.vlist_ref, bf16[128,1024]{1,0:T(8,128)(2,1)} %copy-done.7, ...), custom_call_target="tpu_custom_call" | custom-call | tf_op jit(solution)/shard_map/block_attention/pallas_call | solution.py:113
  73.8 9.6 %collective-permute-start.5 = (bf16[8,128,128]{2,1,0:T(8,128)(2,1)}, bf16[8,128,128]{2,1,0:T(8,128)(2,1)S(1)}, u32[]{:S(2)}, u32[]{:S(2)}) collective-permute-start(bf16[8,128,128]{2,1,0:T(8,128)(2,1)} %get-tuple-element.21), channel_id=1, source_target_pairs={{0,24},{2,26},{4,28},{6,30},{8,0},{10,2},{12,4},{14,6},{16,8},{18,... | collective-permute-start | bytes 786440 | tf_op jit(solution)/shard_map/ppermute | solution.py:207
  84.1 8.0 %block_attention.6 = (bf16[8,128,128]{2,1,0:T(8,128)(2,1)}, f32[8,128]{1,0:T(8,128)}) custom-call(s32[1]{0:T(128)} %constant.83.clone.1.turn_ref, s32[32]{0:T(128)} %reshape.129.count_ref, s32[4]{0:T(128)} %and_select_fusion.diag_ref, s32[1024]{0:T(1024)} %copy-done.12, s32[1024]{0:T(1024)} %broadcast_select_fusion.vlist_ref, bf16[128,1024]{1,0:T(8,128)(2,1)} %copy-done.6, ...), custom_call_target="tpu_custom_call" | custom-call | tf_op jit(solution)/shard_map/block_attention/pallas_call | solution.py:113
  92.1 2.5 %collective-permute-start.3 = (bf16[8,128,128]{2,1,0:T(8,128)(2,1)}, bf16[8,128,128]{2,1,0:T(8,128)(2,1)S(1)}, u32[]{:S(2)}, u32[]{:S(2)}) collective-permute-start(bf16[8,128,128]{2,1,0:T(8,128)(2,1)} %get-tuple-element.20), channel_id=1, source_target_pairs={{0,16},{2,18},{4,20},{6,22},{8,24},{10,26},{12,28},{14,30},{16,0},... | collective-permute-start | bytes 786440 | tf_op jit(solution)/shard_map/ppermute | solution.py:207
  95.4 8.0 %block_attention.5 = (bf16[8,128,128]{2,1,0:T(8,128)(2,1)}, f32[8,128]{1,0:T(8,128)}) custom-call(s32[1]{0:T(128)} %constant.82.clone.1.turn_ref, s32[32]{0:T(128)} %reshape.129.count_ref, s32[4]{0:T(128)} %and_select_fusion.diag_ref, s32[1024]{0:T(1024)} %copy-done.12, s32[1024]{0:T(1024)} %broadcast_select_fusion.vlist_ref, bf16[128,1024]{1,0:T(8,128)(2,1)} %copy-done.5, ...), custom_call_target="tpu_custom_call" | custom-call | tf_op jit(solution)/shard_map/block_attention/pallas_call | solution.py:113
  103.4 9.8 %collective-permute-start.1 = (bf16[8,128,128]{2,1,0:T(8,128)(2,1)}, bf16[8,128,128]{2,1,0:T(8,128)(2,1)S(1)}, u32[]{:S(2)}, u32[]{:S(2)}) collective-permute-start(bf16[8,128,128]{2,1,0:T(8,128)(2,1)} %get-tuple-element.19), channel_id=1, source_target_pairs={{0,8},{2,10},{4,12},{6,14},{8,16},{10,18},{12,20},{14,22},{16,24},... | collective-permute-start | bytes 786440 | tf_op jit(solution)/shard_map/ppermute | solution.py:207
  113.1 8.3 %collective-permute-start.8 = (f32[8,128]{1,0:T(8,128)S(1)}, f32[8,128]{1,0:T(8,128)S(1)}, u32[]{:S(2)}, u32[]{:S(2)}) collective-permute-start(f32[8,128]{1,0:T(8,128)S(1)} %copy-done.17), channel_id=1, source_target_pairs={{0,24},{2,26},{4,28},{6,30},{8,0},{10,2},{12,4},{14,6},{16,8},{18,... | collective-permute-start | bytes 12296 | tf_op jit(solution)/shard_map/ppermute | solution.py:207
  122.8 1.7 collective-permute-start.6
  124.5 8.2 %block_attention.4 = (bf16[8,128,128]{2,1,0:T(8,128)(2,1)}, f32[8,128]{1,0:T(8,128)}) custom-call(s32[1]{0:T(128)} %constant.69.clone.1.turn_ref, s32[32]{0:T(128)} %reshape.129.count_ref, s32[4]{0:T(128)} %and_select_fusion.diag_ref, s32[1024]{0:T(1024)} %copy-done.12, s32[1024]{0:T(1024)} %broadcast_select_fusion.vlist_ref, bf16[128,1024]{1,0:T(8,128)(2,1)} %bitcast.89, ...), custom_call_target="tpu_custom_call" | custom-call | tf_op jit(solution)/shard_map/block_attention/pallas_call | solution.py:113
  133.6 2.2 %combine.1 = bf16[128,1024]{1,0:T(8,128)(2,1)} custom-call(bf16[8,128,128]{2,1,0:T(8,128)(2,1)} %get-tuple-element.18.refs_0_, bf16[8,128,128]{2,1,0:T(8,128)(2,1)} %copy-done.11, bf16[8,128,128]{2,1,0:T(8,128)(2,1)} %copy-done.10, bf16[8,128,128]{2,1,0:T(8,128)(2,1)} %copy-done.9, f32[8,128]{1,0:T(8,128)} %get-tuple-element.22.refs_4_, ...), custom_call_target="tpu_custom_call" | custom-call | tf_op jit(solution)/shard_map/combine/pallas_call | solution.py:156
  135.8 13.1 %collective-permute-start.9 = (bf16[128,1024]{1,0:T(8,128)(2,1)}, bf16[128,1024]{1,0:T(8,128)(2,1)S(1)}, u32[]{:S(2)}, u32[]{:S(2)}) collective-permute-start(bf16[128,1024]{1,0:T(8,128)(2,1)} %combine.1), channel_id=1, source_target_pairs={{0,24},{2,26},{4,28},{6,30},{8,0},{10,2},{12,4},{14,6},{16,8},{18,... | collective-permute-start | bytes 786440 | tf_op jit(solution)/shard_map/ppermute | solution.py:207
  158.9 15.6 %collective-permute-done.10 = bf16[128,1024]{1,0:T(8,128)(2,1)S(1)} collective-permute-done((bf16[128,1024]{1,0:T(8,128)(2,1)}, bf16[128,1024]{1,0:T(8,128)(2,1)S(1)}, u32[]{:S(2)}, u32[]{:S(2)}) %collective-permute-start.10) | collective-permute-done | bytes 262176 | tf_op jit(solution)/shard_map/ppermute | solution.py:207
  177.9 1.7 fusion.3
  188.5 17.5 %all_to_all.25 = bf16[4,256,512]{2,1,0:T(8,128)(2,1)S(1)} all-to-all(bf16[4,256,512]{2,1,0:T(8,128)(2,1)S(1)} %fusion), channel_id=1, replica_groups={{0,2,4,6},{8,10,12,14},{16,18,20,22},{24,26,28,30},{1,3,5,7},{9,11,13,1..., dimensions={0} | all-to-all | bytes 2097152 | tf_op jit(solution)/shard_map/all_to_all | solution.py:253
  (94 shorter events, 30.4 us)
Async XLA Ops:
  0.0 51.6 %copy-start = (s32[32,48]{1,0:T(8,128)S(1)}, s32[32,48]{1,0:T(8,128)}, u32[]{:S(2)}) copy-start(s32[32,48]{1,0:T(8,128)} %param.10) | copy-start | bytes 18436
  0.0 24.8 %copy-start.13 = (s32[32,8]{0,1:T(8,128)S(1)}, s32[32,8]{0,1:T(8,128)}, u32[]{:S(2)}) copy-start(s32[32,8]{0,1:T(8,128)} %param.9) | copy-start | bytes 3076
  0.0 25.0 %copy-start.8 = (bf16[32,4096]{1,0:T(8,128)(2,1)S(1)}, bf16[32,4096]{1,0:T(8,128)(2,1)}, u32[]{:S(2)}) copy-start(bf16[32,4096]{1,0:T(8,128)(2,1)} %param.6) | copy-start | bytes 786436
  2.4 18.8 %all-to-all-start.1 = ((bf16[4,1024,128]{2,1,0:T(8,128)(2,1)}), bf16[4,1024,128]{2,1,0:T(8,128)(2,1)S(1)}, u32[]{:S(2)}, u32[]{:S(2)}) async-start(bf16[4,1024,128]{2,1,0:T(8,128)(2,1)} %bitcast.77), calls=%async_computation.1 | async-start | bytes 2097152 | tf_op jit(solution)/shard_map/all_to_all | solution.py:211
  21.3 25.4 %copy-start.1 = (bf16[4,1024,128]{2,1,0:T(8,128)(2,1)}, bf16[4,1024,128]{2,1,0:T(8,128)(2,1)S(1)}, u32[]{:S(2)}) copy-start(bf16[4,1024,128]{2,1,0:T(8,128)(2,1)S(1)} %all-to-all-done.1) | copy-start | bytes 3145732
  21.3 16.6 %all-to-all-start.2 = ((bf16[4,1024,128]{2,1,0:T(8,128)(2,1)}), bf16[4,1024,128]{2,1,0:T(8,128)(2,1)S(1)}, u32[]{:S(2)}, u32[]{:S(2)}) async-start(bf16[4,1024,128]{2,1,0:T(8,128)(2,1)} %bitcast.76), calls=%async_computation.2 | async-start | bytes 2097152 | tf_op jit(solution)/shard_map/all_to_all | solution.py:212
  37.9 8.8 %all-to-all-start = ((bf16[4,32,1024]{2,1,0:T(8,128)(2,1)}), bf16[4,32,1024]{2,1,0:T(8,128)(2,1)S(1)}, u32[]{:S(2)}, u32[]{:S(2)}) async-start(bf16[4,32,1024]{2,1,0:T(8,128)(2,1)} %bitcast.79), calls=%async_computation | async-start | bytes 524288 | tf_op jit(solution)/shard_map/all_to_all | solution.py:209
  46.7 11.7 %copy-start.3 = (bf16[4,32,1024]{2,1,0:T(8,128)(2,1)}, bf16[4,32,1024]{2,1,0:T(8,128)(2,1)S(1)}, u32[]{:S(2)}) copy-start(bf16[4,32,1024]{2,1,0:T(8,128)(2,1)S(1)} %all-to-all-done) | copy-start | bytes 786436
  46.7 127.9 %all-to-all-start.3 = ((bf16[4,1024,512]{2,1,0:T(8,128)(2,1)}), bf16[4,1024,512]{2,1,0:T(8,128)(2,1)}, u32[]{:S(2)}, u32[]{:S(2)}) async-start(bf16[4,1024,512]{2,1,0:T(8,128)(2,1)} %bitcast.84), calls=%async_computation.3 | async-start | bytes 8388608 | tf_op jit(solution)/shard_map/all_to_all | solution.py:214
  54.1 11.0 %collective-permute-start.4 = (bf16[128,1024]{1,0:T(8,128)(2,1)S(1)}, bf16[128,1024]{1,0:T(8,128)(2,1)S(1)}, u32[]{:S(2)}, u32[]{:S(2)}) collective-permute-start(bf16[128,1024]{1,0:T(8,128)(2,1)S(1)} %bitcast.86), channel_id=1, source_target_pairs={{0,8},{2,10},{4,12},{6,14},{8,16},{10,18},{12,20},{14,22},{16,24},... | collective-permute-start | bytes 786440 | tf_op jit(solution)/shard_map/ppermute | solution.py:207
  55.7 27.7 %collective-permute-start.2 = (bf16[128,1024]{1,0:T(8,128)(2,1)S(1)}, bf16[128,1024]{1,0:T(8,128)(2,1)S(1)}, u32[]{:S(2)}, u32[]{:S(2)}) collective-permute-start(bf16[128,1024]{1,0:T(8,128)(2,1)S(1)} %bitcast.87), channel_id=1, source_target_pairs={{0,16},{2,18},{4,20},{6,22},{8,24},{10,26},{12,28},{14,30},{16,0},... | collective-permute-start | bytes 786440 | tf_op jit(solution)/shard_map/ppermute | solution.py:207
  58.3 36.4 %collective-permute-start = (bf16[128,1024]{1,0:T(8,128)(2,1)S(1)}, bf16[128,1024]{1,0:T(8,128)(2,1)S(1)}, u32[]{:S(2)}, u32[]{:S(2)}) collective-permute-start(bf16[128,1024]{1,0:T(8,128)(2,1)S(1)} %bitcast.88), channel_id=1, source_target_pairs={{0,24},{2,26},{4,28},{6,30},{8,0},{10,2},{12,4},{14,6},{16,8},{18,... | collective-permute-start | bytes 786440 | tf_op jit(solution)/shard_map/ppermute | solution.py:207
  73.8 39.3 %copy-start.17 = (f32[8,128]{1,0:T(8,128)S(1)}, f32[8,128]{1,0:T(8,128)}, u32[]{:S(2)}) copy-start(f32[8,128]{1,0:T(8,128)} %get-tuple-element.25) | copy-start | bytes 12292
  73.8 58.9 %collective-permute-start.5 = (bf16[8,128,128]{2,1,0:T(8,128)(2,1)}, bf16[8,128,128]{2,1,0:T(8,128)(2,1)S(1)}, u32[]{:S(2)}, u32[]{:S(2)}) collective-permute-start(bf16[8,128,128]{2,1,0:T(8,128)(2,1)} %get-tuple-element.21), channel_id=1, source_target_pairs={{0,24},{2,26},{4,28},{6,30},{8,0},{10,2},{12,4},{14,6},{16,8},{18,... | collective-permute-start | bytes 786440 | tf_op jit(solution)/shard_map/ppermute | solution.py:207
  92.1 40.6 %collective-permute-start.3 = (bf16[8,128,128]{2,1,0:T(8,128)(2,1)}, bf16[8,128,128]{2,1,0:T(8,128)(2,1)S(1)}, u32[]{:S(2)}, u32[]{:S(2)}) collective-permute-start(bf16[8,128,128]{2,1,0:T(8,128)(2,1)} %get-tuple-element.20), channel_id=1, source_target_pairs={{0,16},{2,18},{4,20},{6,22},{8,24},{10,26},{12,28},{14,30},{16,0},... | collective-permute-start | bytes 786440 | tf_op jit(solution)/shard_map/ppermute | solution.py:207
  103.4 29.3 %collective-permute-start.1 = (bf16[8,128,128]{2,1,0:T(8,128)(2,1)}, bf16[8,128,128]{2,1,0:T(8,128)(2,1)S(1)}, u32[]{:S(2)}, u32[]{:S(2)}) collective-permute-start(bf16[8,128,128]{2,1,0:T(8,128)(2,1)} %get-tuple-element.19), channel_id=1, source_target_pairs={{0,8},{2,10},{4,12},{6,14},{8,16},{10,18},{12,20},{14,22},{16,24},... | collective-permute-start | bytes 786440 | tf_op jit(solution)/shard_map/ppermute | solution.py:207
  113.1 9.7 %collective-permute-start.8 = (f32[8,128]{1,0:T(8,128)S(1)}, f32[8,128]{1,0:T(8,128)S(1)}, u32[]{:S(2)}, u32[]{:S(2)}) collective-permute-start(f32[8,128]{1,0:T(8,128)S(1)} %copy-done.17), channel_id=1, source_target_pairs={{0,24},{2,26},{4,28},{6,30},{8,0},{10,2},{12,4},{14,6},{16,8},{18,... | collective-permute-start | bytes 12296 | tf_op jit(solution)/shard_map/ppermute | solution.py:207
  121.5 11.2 %collective-permute-start.7 = (f32[8,128]{1,0:T(8,128)}, f32[8,128]{1,0:T(8,128)S(1)}, u32[]{:S(2)}, u32[]{:S(2)}) collective-permute-start(f32[8,128]{1,0:T(8,128)} %get-tuple-element.24), channel_id=1, source_target_pairs={{0,16},{2,18},{4,20},{6,22},{8,24},{10,26},{12,28},{14,30},{16,0},... | collective-permute-start | bytes 12296 | tf_op jit(solution)/shard_map/ppermute | solution.py:207
  122.8 9.9 %copy-start.14 = (f32[8,128]{1,0:T(8,128)}, f32[8,128]{1,0:T(8,128)S(1)}, u32[]{:S(2)}) copy-start(f32[8,128]{1,0:T(8,128)S(1)} %collective-permute-done.8.refs_7_) | copy-start | bytes 12292
  122.8 9.9 %collective-permute-start.6 = (f32[8,128]{1,0:T(8,128)}, f32[8,128]{1,0:T(8,128)S(1)}, u32[]{:S(2)}, u32[]{:S(2)}) collective-permute-start(f32[8,128]{1,0:T(8,128)} %get-tuple-element.23), channel_id=1, source_target_pairs={{0,8},{2,10},{4,12},{6,14},{8,16},{10,18},{12,20},{14,22},{16,24},... | collective-permute-start | bytes 12296 | tf_op jit(solution)/shard_map/ppermute | solution.py:207
  135.8 23.1 %collective-permute-start.9 = (bf16[128,1024]{1,0:T(8,128)(2,1)}, bf16[128,1024]{1,0:T(8,128)(2,1)S(1)}, u32[]{:S(2)}, u32[]{:S(2)}) collective-permute-start(bf16[128,1024]{1,0:T(8,128)(2,1)} %combine.1), channel_id=1, source_target_pairs={{0,24},{2,26},{4,28},{6,30},{8,0},{10,2},{12,4},{14,6},{16,8},{18,... | collective-permute-start | bytes 786440 | tf_op jit(solution)/shard_map/ppermute | solution.py:207
  157.1 17.4 %collective-permute-start.10 = (bf16[128,1024]{1,0:T(8,128)(2,1)}, bf16[128,1024]{1,0:T(8,128)(2,1)S(1)}, u32[]{:S(2)}, u32[]{:S(2)}) collective-permute-start(bf16[128,1024]{1,0:T(8,128)(2,1)} %combine.1), channel_id=1, source_target_pairs={{0,16},{2,18},{4,20},{6,22},{8,24},{10,26},{12,28},{14,30},{16,0},... | collective-permute-start | bytes 786440 | tf_op jit(solution)/shard_map/ppermute | solution.py:207
  157.2 17.3 %collective-permute-start.11 = (bf16[128,1024]{1,0:T(8,128)(2,1)}, bf16[128,1024]{1,0:T(8,128)(2,1)S(1)}, u32[]{:S(2)}, u32[]{:S(2)}) collective-permute-start(bf16[128,1024]{1,0:T(8,128)(2,1)} %combine.1), channel_id=1, source_target_pairs={{0,8},{2,10},{4,12},{6,14},{8,16},{10,18},{12,20},{14,22},{16,24},... | collective-permute-start | bytes 786440 | tf_op jit(solution)/shard_map/ppermute | solution.py:207
  181.4 6.8 %collective-permute-start.12 = (bf16[4,256,512]{2,1,0:T(8,128)(2,1)S(1)}, bf16[4,256,512]{2,1,0:T(8,128)(2,1)S(1)}, u32[]{:S(2)}, u32[]{:S(2)}) collective-permute-start(bf16[4,256,512]{2,1,0:T(8,128)(2,1)S(1)} %pad_maximum_fusion), channel_id=1, source_target_pairs={{0,1},{1,0},{2,3},{3,2},{4,5},{5,4},{6,7},{7,6},{8,9},{9,8},{10,11... | collective-permute-start | bytes 3145736 | tf_op jit(solution)/shard_map/ppermute | solution.py:248
  (11 other events, 26.1 us)
